TPU v7x, 128 devices: a whole 4x4x4 slice. The times are simulated.
128 devices in a mesh: leaf: 16 (over x, z), panel: 8 (over y, core).
Axes of the slice: x: 4, y: 4, z: 4, core: 2. Of those that a mesh axis runs over, the one named last changes fastest.
Arguments:
- adjoint_rhs: float32 [16, 64, 3968], P('leaf', None, 'panel'), may hold values from -6 to 6
- panel_tiles: bfloat16 [16, 2048, 12544], P('leaf', 'panel'), may hold values from -0.0625 to 0.0625
- diag_inverse: bfloat16 [16, 3968, 2048], P('leaf', 'panel'), may hold values from -0.125 to 0.125
- front_sizes: int32 [31], replicated, may hold values from 512 to 2048
Outputs:
- solution: float32 [16, 5, 64, 2048], P('leaf', None, None, 'panel')
All inputs are finite; a program needn't handle non-finite values.
Results may differ from a plain program's by a relative error of at most 0.0051.
Values sent between devices are 32-bit elements; how exact they have to be, the bound alone decides.
A program may use at most 128 MiB of HBM per device.

v0:
```python
import jax
import jax.numpy as jnp
from jax import lax
from jax.sharding import PartitionSpec as P


def per_device(adjoint_rhs, panel_tiles, diag_inverse, front_sizes):
    leaf_count = lax.axis_size("leaf")
    panel_count = lax.axis_size("panel")
    levels = leaf_count.bit_length()
    leaf_pos = lax.axis_index("leaf")
    panel_pos = lax.axis_index("panel")
    sep_rows = diag_inverse.shape[2]
    strip = panel_tiles.shape[1]
    columns = jnp.arange(sep_rows)
    solved = []
    results = []
    for height in range(levels):
        group_size = leaf_count >> height
        col_width = sep_rows // group_size
        share = col_width // panel_count
        col_start = sum((upper * (sep_rows // (leaf_count >> upper)) for upper in range(height)))
        row_start = sum(
            (sep_rows // (leaf_count >> upper) // panel_count for upper in range(height))
        )
        front_pos = leaf_pos // group_size
        member = leaf_pos % group_size
        right = adjoint_rhs[0, :, row_start : row_start + share]
        if height > 0:
            strips = jnp.stack([solved[upper] for upper in range(height)], axis=1)
            region = panel_tiles[0, :, col_start : col_start + height * col_width].reshape(
                strip, height, col_width
            )
            partial_value = jnp.einsum(
                "nar,raw->nw", strips, region, preferred_element_type=jnp.float32
            )
            shares = lax.psum_scatter(partial_value, "panel", scatter_dimension=1, tiled=True)
            resid = right - shares
        else:
            resid = right
        front_id = (1 << height) - 1 + front_pos
        live_size = jnp.sum(jnp.where(jnp.arange(front_sizes.shape[0]) == front_id, front_sizes, 0))
        global_rows = member * col_width + panel_pos * share + jnp.arange(share)
        resid_low = jnp.where(global_rows[None, :] < live_size, resid, 0.0).astype(jnp.bfloat16)
        block = diag_inverse[0, row_start : row_start + share, :].astype(jnp.float32)
        below = columns[None, :] <= global_rows[:, None]
        factor = (
            jnp.where(below, block, 0.0)
            + (columns[None, :] == global_rows[:, None]).astype(jnp.float32)
        ).astype(jnp.bfloat16)
        terms = jnp.dot(resid_low, factor, preferred_element_type=jnp.float32)
        slots = jnp.zeros((leaf_count // group_size,) + terms.shape, jnp.float32)
        slots = lax.dynamic_update_index_in_dim(slots, terms, front_pos, 0)
        summed = lax.psum(slots, ("leaf", "panel"))
        total = lax.dynamic_index_in_dim(summed, front_pos, 0, keepdims=False)
        mine = lax.dynamic_slice_in_dim(total, panel_pos * strip, strip, 1)
        rows_now = mine.astype(jnp.bfloat16)
        solved.append(rows_now)
        results.append(mine)
    return jnp.stack(results, axis=0)[None]


def solution(mesh):
    in_specs = (P("leaf", None, "panel"), P("leaf", "panel", None), P("leaf", "panel", None), P())
    out_specs = P("leaf", None, None, "panel")
    return jax.shard_map(
        per_device, mesh=mesh, in_specs=in_specs, out_specs=out_specs, check_vma=False
    )
```

profile of v0, /device:TPU:1, one launch (start us, length us, event | category | flops | bytes accessed | tf_op | source)
XLA Modules:
  0.0 927.9 jit_solution(10410377845542587859)
XLA Ops:
  6.5 1.5 fusion.88
  8.7 1.9 convolution_bitcast_fusion
  10.7 150.0 %all-reduce.6.cloned.1.call-done = f32[1,64,2048]{2,1,0:T(8,128)} async-done(((f32[1,64,2048]{2,1,0:T(8,128)}), f32[1,64,2048]{2,1,0:T(8,128)}) %all-reduce.6.cloned.1.call-update) | async-done | bytes 524304 | tf_op jit(solution)/shard_map/psum | solution.py:54
  160.7 1.8 convolution_bitcast_fusion.8
  163.3 26.0 %reduce-scatter.13.cloned.1.call-done = f32[32,64]{1,0:T(8,128)} async-done(((f32[256,64]{1,0:T(8,128)}), f32[32,64]{1,0:T(8,128)}) %reduce-scatter.13.cloned.1.call-update) | async-done | bytes 8208
  190.3 1.2 fusion.2
  193.6 149.4 %all-reduce.8.cloned.1.call-done = f32[2,64,2048]{2,1,0:T(8,128)} async-done(((f32[2,64,2048]{2,1,0:T(8,128)}), f32[2,64,2048]{2,1,0:T(8,128)}) %all-reduce.8.cloned.1.call-update) | async-done | bytes 1048592 | tf_op jit(solution)/shard_map/psum | solution.py:54
  345.8 26.0 %reduce-scatter.15.cloned.1.call-done = f32[64,64]{1,0:T(8,128)} async-done(((f32[512,64]{1,0:T(8,128)}), f32[64,64]{1,0:T(8,128)}) %reduce-scatter.15.cloned.1.call-update) | async-done | bytes 16400
  372.9 1.3 fusion.1
  374.2 1.3 copy-done
  375.7 1.3 slice-done.1
  377.7 150.7 %all-reduce.10.cloned.1.call-done = f32[4,64,2048]{2,1,0:T(8,128)} async-done(((f32[4,64,2048]{2,1,0:T(8,128)}), f32[4,64,2048]{2,1,0:T(8,128)}) %all-reduce.10.cloned.1.call-update) | async-done | bytes 2097168 | tf_op jit(solution)/shard_map/psum | solution.py:54
  529.3 1.3 convolution_bitcast_fusion.7
  531.5 25.5 %reduce-scatter.9.cloned.1.call-done = f32[64,128]{1,0:T(8,128)} async-done(((f32[64,1024]{1,0:T(8,128)}), f32[64,128]{1,0:T(8,128)}) %reduce-scatter.9.cloned.1.call-update) | async-done | bytes 32784 | tf_op jit(solution)/shard_map/reduce_scatter | solution.py:37
  557.0 2.5 broadcast_in_dim.164
  559.4 1.3 fusion
  560.8 4.6 slice.54
  565.4 6.4 copy.26
  571.8 146.6 %all-reduce.12.cloned.1.call-done = f32[8,64,2048]{2,1,0:T(8,128)} async-done(((f32[8,64,2048]{2,1,0:T(8,128)}), f32[8,64,2048]{2,1,0:T(8,128)}) %all-reduce.12.cloned.1.call-update) | async-done | bytes 4194320 | tf_op jit(solution)/shard_map/psum | solution.py:54
  719.4 4.4 convolution_bitcast_fusion.1
  724.4 25.9 %reduce-scatter.11.cloned.1.call-done = f32[64,256]{1,0:T(8,128)} async-done(((f32[64,2048]{1,0:T(8,128)}), f32[64,256]{1,0:T(8,128)}) %reduce-scatter.11.cloned.1.call-update) | async-done | bytes 65552 | tf_op jit(solution)/shard_map/reduce_scatter | solution.py:37
  750.4 4.3 broadcast_in_dim.169
  754.6 1.6 fusion.3
  760.0 159.6 %all-reduce.14.cloned.1.call-done = f32[16,64,2048]{2,1,0:T(8,128)} async-done(((f32[16,64,2048]{2,1,0:T(8,128)}), f32[16,64,2048]{2,1,0:T(8,128)}) %all-reduce.14.cloned.1.call-update) | async-done | bytes 8388624 | tf_op jit(solution)/shard_map/psum | solution.py:54
  (60 shorter events, 17.9 us)
Async XLA Ops:
  6.5 183.7 %copy-start.2 = (f32[1,64,496]{2,1,0:T(8,128)S(1)}, f32[1,64,496]{2,1,0:T(8,128)}, u32[]{:S(2)}) copy-start(f32[1,64,496]{2,1,0:T(8,128)} %param.4) | copy-start | bytes 380932
  6.5 154.1 %all-reduce.6.cloned.1.call-start = ((), (), s32[]{:S(2)}) async-start(), calls=%async_computation.4 | async-start | bytes 1048576 | tf_op jit(solution)/shard_map/psum | solution.py:54
  10.6 178.7 %reduce-scatter.13.cloned.1.call-start = ((), (), s32[]{:S(2)}) async-start(), calls=%async_computation.11 | async-start | bytes 147456
  162.5 30.1 %slice-start = ((bf16[1,256,12544]{2,1,0:T(8,128)(2,1)}), bf16[1,256,1024]{2,1,0:T(8,128)(2,1)S(1)}, s32[]{:S(2)}) async-start(bf16[1,256,12544]{2,1,0:T(8,128)(2,1)} %param.5), calls=%async_computation.13 | async-start | bytes 1048576 | tf_op jit(solution)/shard_map/slice | solution.py:31
  162.5 180.6 %all-reduce.8.cloned.1.call-start = ((), (), s32[]{:S(2)}) async-start(), calls=%async_computation.5 | async-start | bytes 2097152 | tf_op jit(solution)/shard_map/psum | solution.py:54
  191.5 1.0 copy-start.1
  192.5 179.3 %reduce-scatter.15.cloned.1.call-start = ((), (), s32[]{:S(2)}) async-start(), calls=%async_computation.12 | async-start | bytes 294912
  345.1 183.3 %all-reduce.10.cloned.1.call-start = ((), (), s32[]{:S(2)}) async-start(), calls=%async_computation.6 | async-start | bytes 4194304 | tf_op jit(solution)/shard_map/psum | solution.py:54
  374.2 1.4 copy-start
  375.6 1.4 slice-start.1
  375.6 181.4 %reduce-scatter.9.cloned.1.call-start = ((), (), s32[]{:S(2)}) async-start(), calls=%async_computation.7 | async-start | bytes 294912 | tf_op jit(solution)/shard_map/reduce_scatter | solution.py:37
  530.7 187.7 %all-reduce.12.cloned.1.call-start = ((), (), s32[]{:S(2)}) async-start(), calls=%async_computation.8 | async-start | bytes 8388608 | tf_op jit(solution)/shard_map/psum | solution.py:54
  531.4 28.0 %copy-start.3 = (bf16[1,496,2048]{2,1,0:T(8,128)(2,1)S(1)}, bf16[1,496,2048]{2,1,0:T(8,128)(2,1)}, u32[]{:S(2)}) copy-start(bf16[1,496,2048]{2,1,0:T(8,128)(2,1)} %param.6) | copy-start | bytes 6094852
  556.9 2.5 copy-start.6
  560.7 189.6 %reduce-scatter.11.cloned.1.call-start = ((), (), s32[]{:S(2)}) async-start(), calls=%async_computation.9 | async-start | bytes 589824 | tf_op jit(solution)/shard_map/reduce_scatter | solution.py:37
  723.7 195.9 %all-reduce.14.cloned.1.call-start = ((), (), s32[]{:S(2)}) async-start(), calls=%async_computation.10 | async-start | bytes 16777216 | tf_op jit(solution)/shard_map/psum | solution.py:54
  750.4 4.3 copy-start.5
  920.7 0.7 copy-start.4
Sparse Core Ops, SparseCore 0:
  12.1 148.5 all-reduce.5
  163.1 26.1 reduce-scatter.12
  194.2 148.8 all-reduce.7
  345.4 26.3 reduce-scatter.14
  376.5 151.8 all-reduce.9
  530.8 26.1 reduce-scatter.8
  562.6 155.7 all-reduce.11
  723.9 26.4 reduce-scatter.10
  756.4 163.2 all-reduce.13
where the time goes:
time: 929 us; the launch traced here: 928 us
  waiting for transfers between devices  860 us (93%)
  local copies, waits for them, and re-layouts  33.5 us (4%)
  matrix products  15.8 us (2%)
  between operations  13.5 us (1%)
    psum x5, waiting for transfers between devices, per_device(): summed = lax.psum(slots, ('leaf', 'panel'))  756 us
    unnamed x11, waiting for transfers between devices  52.2 us
    reduce_scatter x2, waiting for transfers between devices, per_device(): lax.psum_scatter(partial_value, 'panel', scatter_dimension=1, tiled=True)  51.4 us
  transfers between devices with their start and end apart: 9, of which 9 were waited for; matrix products, arithmetic and copies ran while one was open for 2% of the time, Pallas kernels for 0%

commit v1 on v0

v1 whole, which is shorter than its diff:
```python
import jax
import jax.numpy as jnp
from jax import lax
from jax.experimental import pallas as pl
from jax.experimental.pallas import tpu as pltpu
from jax.sharding import PartitionSpec as P

MESH = pl.DeviceIdType.MESH
F32, BF16 = jnp.float32, jnp.bfloat16
NP = 8
NL = 16
SEP = 2048
N = 64
STRIP = SEP // NP
LEVELS = 5
G = [NL >> lev for lev in range(LEVELS)]
W = [SEP // g for g in G]
V = [w // NP for w in W]
C = [sum(m * W[m] for m in range(lev)) for lev in range(LEVELS)]
R = [sum(V[m] for m in range(lev)) for lev in range(LEVELS)]
TILES = N // 8 * (STRIP // 128)
GATHER = (0, 1, 2)
SPREAD = (3, 4)
TWO_STEP = (0, 1, 2)


def kernel(*refs):
    refs = list(refs)
    sizes, rhs_hbm, tiles_hbm, diag_hbm, out = refs[:5]
    names = [name for name, _ in scratch()]
    s = dict(zip(names, refs[5:], strict=True))
    me_leaf, me = lax.axis_index("leaf"), lax.axis_index("panel")

    def panel_peer(k):
        return {"panel": lax.rem(me + k, NP)}, lax.rem(me + k, NP)

    def member(lev):
        return lax.rem(me_leaf, G[lev])

    def leaf_peer(lev, k):
        d = member(lev)
        to = lax.rem(d + k, G[lev])
        return {"leaf": me_leaf - d + to}, to

    loads = {}
    done = set()

    def loaded(name):
        if name not in done:
            done.add(name)
            loads[name].wait()

    def load(name, src, dst):
        loads[name] = pltpu.make_async_copy(src, dst, s["load_sem"].at[len(loads)])
        loads[name].start()

    load("rhs", rhs_hbm.at[0], s["rhs"])
    for lev in range(LEVELS):
        rows = pl.ds(R[lev], V[lev])
        load(("diag", lev), diag_hbm.at[0, rows, :], s["diag"].at[rows, :])
        if lev:
            cols = pl.ds(C[lev], lev * W[lev])
            load(("tiles", lev), tiles_hbm.at[0, :, cols], s["tiles"].at[:, cols])

    barrier = pltpu.get_barrier_semaphore()
    for k in range(1, NP):
        pl.semaphore_signal(barrier, inc=1, device_id=panel_peer(k)[0], device_id_type=MESH)
    for k in range(1, NL):
        pl.semaphore_signal(barrier, inc=1, device_id=leaf_peer(0, k)[0], device_id_type=MESH)

    sent = []

    def send(tag, k, src, dst, device):
        copy = pltpu.make_async_remote_copy(
            src_ref=src,
            dst_ref=dst,
            send_sem=s[tag + "_ssem"].at[k - 1],
            recv_sem=s[tag + "_rsem"].at[k - 1],
            device_id=device,
            device_id_type=MESH,
        )
        copy.start()
        sent.append(copy)
        return copy

    def arrive(copies):
        for copy in copies:
            copy.wait_recv()

    def factor_rows(lev):
        loaded(("diag", lev))
        block = s["diag"][R[lev] : R[lev] + V[lev], :].astype(F32)
        row = lax.broadcasted_iota(jnp.int32, (V[lev], SEP), 0)
        row = row + (member(lev) * W[lev] + me * V[lev])
        col = lax.broadcasted_iota(jnp.int32, (V[lev], SEP), 1)
        return jnp.where(col <= row, block, 0.0) + jnp.where(col == row, 1.0, 0.0)

    def send_factor(lev):
        full = factor_rows(lev)
        for q in range(NP):
            s[f"msend{lev}"][q] = full[:, q * STRIP : (q + 1) * STRIP]
        copies = []
        for k in range(1, NP):
            device, to = panel_peer(k)
            copies.append(
                send(f"m{lev}", k, s[f"msend{lev}"].at[to], s[f"mfull{lev}"].at[me], device)
            )
        s[f"mfull{lev}"][me] = s[f"msend{lev}"][me]
        return copies

    def live(lev):
        return sizes[(1 << lev) - 1 + lax.div(me_leaf, G[lev])]

    def put_tiles(ref, value):
        for row in range(N // 8):
            for half in range(STRIP // 128):
                ref[row * 2 + half] = value[row * 8 : row * 8 + 8, half * 128 : half * 128 + 128]

    def get_tiles(ref):
        rows = [
            jnp.concatenate([ref[row * 2], ref[row * 2 + 1]], axis=1) for row in range(N // 8)
        ]
        return jnp.concatenate(rows, axis=0)

    def leaf_sum(lev, value, beside, beside2):
        g, d = G[lev], member(lev)
        if g == 1:
            return value
        if lev not in TWO_STEP:
            s[f"xs{lev}"][...] = value
            copies = []
            for k in range(1, g):
                device, _ = leaf_peer(lev, k)
                copies.append(send(f"xs{lev}", k, s[f"xs{lev}"], s[f"xr{lev}"].at[k - 1], device))
            beside()
            beside2()
            arrive(copies)
            total = value
            for k in range(1, g):
                total = total + s[f"xr{lev}"][k - 1]
            return total
        t = TILES // g
        put_tiles(s[f"xs{lev}"], value)
        copies = []
        for k in range(1, g):
            device, to = leaf_peer(lev, k)
            copies.append(
                send(
                    f"xs{lev}",
                    k,
                    s[f"xs{lev}"].at[pl.ds(to * t, t)],
                    s[f"xr{lev}"].at[k - 1],
                    device,
                )
            )
        beside()
        arrive(copies)
        total = s[f"xs{lev}"][pl.ds(d * t, t)]
        for k in range(1, g):
            total = total + s[f"xr{lev}"][k - 1]
        s[f"xf{lev}"][pl.ds(d * t, t)] = total
        copies = []
        for k in range(1, g):
            device, _ = leaf_peer(lev, k)
            here = s[f"xf{lev}"].at[pl.ds(d * t, t)]
            copies.append(send(f"xf{lev}", k, here, here, device))
        beside2()
        arrive(copies)
        return get_tiles(s[f"xf{lev}"])

    def tile_of(lev, upper):
        start = C[lev] + upper * W[lev]
        return s["tiles"][:, start : start + W[lev]]

    def term(lev, upper, x):
        return jnp.dot(x, tile_of(lev, upper), preferred_element_type=F32)

    def placed_rhs(lev):
        y = s["rhs"][:, R[lev] : R[lev] + V[lev]]
        spread = jnp.concatenate([y] * NP, axis=1)
        col = lax.broadcasted_iota(jnp.int32, (N, W[lev]), 1)
        first = me * V[lev]
        return jnp.where((col >= first) & (col < first + V[lev]), spread, 0.0)

    def nothing():
        pass

    loaded("rhs")
    z = s["rhs"][:, : V[0]]
    col = lax.broadcasted_iota(jnp.int32, (N, V[0]), 1) + (member(0) * W[0] + me * V[0])
    z = jnp.where(col < live(0), z, 0.0)
    s["zs0"][...] = jnp.concatenate([z[8 * r : 8 * r + 8, :] for r in range(N // 8)], axis=1)
    pl.semaphore_wait(barrier, NP - 1 + NL - 1)
    z_copies = []
    for k in range(1, NP):
        device, _ = panel_peer(k)
        z_copies.append(send("zf0", k, s["zs0"], s["zf0"].at[me], device))
    s["zf0"][me] = s["zs0"][...]
    m_copies = {0: send_factor(0)}

    def keep_factor(lev):
        s[f"m{lev}"][...] = factor_rows(lev).astype(BF16)

    keep_factor(3)
    arrive(m_copies[0])
    for q in range(NP):
        part = s["mfull0"][q].astype(BF16)
        for r in range(N // 8):
            start = q * 128 + r * V[0]
            s["w0"][start : start + V[0], :] = part
    arrive(z_copies)
    lane = lax.broadcasted_iota(jnp.int32, (N, 128), 1)
    row = lax.broadcasted_iota(jnp.int32, (N, 128), 0)
    own = lax.div(lane, V[0]) == lax.div(row, 8)
    pieces = []
    for q in range(NP):
        spread = jnp.concatenate([s["zf0"][q]] * (N // 8), axis=0)
        pieces.append(jnp.where(own, spread, 0.0).astype(BF16))
    x = jnp.dot(jnp.concatenate(pieces, axis=1), s["w0"][...], preferred_element_type=F32)

    def ahead0():
        m_copies[1] = send_factor(1)

    def ahead0b():
        keep_factor(4)

    x = leaf_sum(0, x, ahead0, ahead0b)
    out[0, 0] = x
    xb = [x.astype(BF16)]

    for lev in range(1, LEVELS):
        loaded(("tiles", lev))
        total = term(lev, lev - 1, xb[lev - 1])
        if lev > 1:
            total = total + s[f"acc{lev}"][...]

        def ahead_terms(lev=lev):
            for later in range(lev + 1, LEVELS):
                loaded(("tiles", later))
                value = term(later, lev - 1, xb[lev - 1])
                if lev > 1:
                    value = value + s[f"acc{later}"][...]
                s[f"acc{later}"][...] = value

        if lev in GATHER:
            part = placed_rhs(lev) - total
            for r in range(NP):
                s[f"zp{lev}"][r] = part[8 * r : 8 * r + 8, :]
            copies = []
            for k in range(1, NP):
                device, to = panel_peer(k)
                copies.append(
                    send(f"zr{lev}", k, s[f"zp{lev}"].at[to], s[f"zr{lev}"].at[k - 1], device)
                )
            ahead_terms()
            arrive(copies)
            rows = s[f"zp{lev}"][me]
            for k in range(1, NP):
                rows = rows + s[f"zr{lev}"][k - 1]
            col = lax.broadcasted_iota(jnp.int32, (8, W[lev]), 1) + member(lev) * W[lev]
            s[f"zf{lev}"][me] = jnp.where(col < live(lev), rows, 0.0)
            copies = []
            for k in range(1, NP):
                device, _ = panel_peer(k)
                here = s[f"zf{lev}"].at[me]
                copies.append(send(f"zf{lev}", k, here, here, device))
            arrive(m_copies[lev])
            weights = s[f"mfull{lev}"][...].reshape(W[lev], STRIP).astype(BF16)
            arrive(copies)
            zb = s[f"zf{lev}"][...].reshape(N, W[lev]).astype(BF16)
            x = jnp.dot(zb, weights, preferred_element_type=F32)
        else:
            for q in range(NP):
                s[f"zp{lev}"][q] = total[:, q * V[lev] : (q + 1) * V[lev]]
            copies = []
            for k in range(1, NP):
                device, to = panel_peer(k)
                copies.append(
                    send(f"zr{lev}", k, s[f"zp{lev}"].at[to], s[f"zr{lev}"].at[k - 1], device)
                )
            ahead_terms()
            arrive(copies)
            rows = s["rhs"][:, R[lev] : R[lev] + V[lev]] - s[f"zp{lev}"][me]
            for k in range(1, NP):
                rows = rows - s[f"zr{lev}"][k - 1]
            col = lax.broadcasted_iota(jnp.int32, (N, V[lev]), 1)
            col = col + (member(lev) * W[lev] + me * V[lev])
            zb = jnp.where(col < live(lev), rows, 0.0).astype(BF16)
            for q in range(NP):
                weights = s[f"m{lev}"][:, q * STRIP : (q + 1) * STRIP]
                s[f"xp{lev}"][q] = jnp.dot(zb, weights, preferred_element_type=F32)
            copies = []
            for k in range(1, NP):
                device, to = panel_peer(k)
                copies.append(
                    send(f"xq{lev}", k, s[f"xp{lev}"].at[to], s[f"xq{lev}"].at[k - 1], device)
                )
            arrive(copies)
            x = s[f"xp{lev}"][me]
            for k in range(1, NP):
                x = x + s[f"xq{lev}"][k - 1]

        def ahead_factor(lev=lev):
            if lev + 1 in GATHER:
                m_copies[lev + 1] = send_factor(lev + 1)

        x = leaf_sum(lev, x, ahead_factor, nothing)
        out[0, lev] = x
        if lev + 1 < LEVELS:
            xb.append(x.astype(BF16))

    for copy in sent:
        copy.wait_send()


def scratch():
    vmem, dma = pltpu.VMEM, pltpu.SemaphoreType.DMA
    found = [
        ("rhs", vmem((N, R[-1] + V[-1]), F32)),
        ("diag", vmem((R[-1] + V[-1], SEP), BF16)),
        ("tiles", vmem((STRIP, C[-1] + (LEVELS - 1) * W[-1]), BF16)),
        ("load_sem", dma((2 * LEVELS,))),
        ("zs0", vmem((8, 128), F32)),
        ("w0", vmem((NP * 128, STRIP), BF16)),
    ]

    def exchange(tag, count):
        found.append((tag + "_ssem", dma((count,))))
        found.append((tag + "_rsem", dma((count,))))

    for lev in GATHER:
        found.append((f"msend{lev}", vmem((NP, V[lev], STRIP), F32)))
        found.append((f"mfull{lev}", vmem((NP, V[lev], STRIP), F32)))
        exchange(f"m{lev}", NP - 1)
        found.append((f"zf{lev}", vmem((NP, 8, 128 if lev == 0 else W[lev]), F32)))
        exchange(f"zf{lev}", NP - 1)
        if lev:
            found.append((f"zp{lev}", vmem((NP, 8, W[lev]), F32)))
            found.append((f"zr{lev}", vmem((NP - 1, 8, W[lev]), F32)))
            exchange(f"zr{lev}", NP - 1)
    for lev in SPREAD:
        found.append((f"m{lev}", vmem((V[lev], SEP), BF16)))
        found.append((f"zp{lev}", vmem((NP, N, V[lev]), F32)))
        found.append((f"zr{lev}", vmem((NP - 1, N, V[lev]), F32)))
        exchange(f"zr{lev}", NP - 1)
        found.append((f"xp{lev}", vmem((NP, N, STRIP), F32)))
        found.append((f"xq{lev}", vmem((NP - 1, N, STRIP), F32)))
        exchange(f"xq{lev}", NP - 1)
    for lev in range(2, LEVELS):
        found.append((f"acc{lev}", vmem((N, W[lev]), F32)))
    for lev in range(LEVELS):
        g = G[lev]
        if g == 1:
            continue
        if lev in TWO_STEP:
            found.append((f"xs{lev}", vmem((TILES, 8, 128), F32)))
            found.append((f"xr{lev}", vmem((g - 1, TILES // g, 8, 128), F32)))
            found.append((f"xf{lev}", vmem((TILES, 8, 128), F32)))
            exchange(f"xf{lev}", g - 1)
        else:
            found.append((f"xs{lev}", vmem((N, STRIP), F32)))
            found.append((f"xr{lev}", vmem((g - 1, N, STRIP), F32)))
        exchange(f"xs{lev}", g - 1)
    return found


def per_device(adjoint_rhs, panel_tiles, diag_inverse, front_sizes):
    anywhere = pl.BlockSpec(memory_space=pl.ANY)
    return pl.pallas_call(
        kernel,
        name="solve",
        out_shape=jax.ShapeDtypeStruct((1, LEVELS, N, STRIP), F32),
        in_specs=[pl.BlockSpec(memory_space=pltpu.SMEM), anywhere, anywhere, anywhere],
        out_specs=pl.BlockSpec(memory_space=pltpu.VMEM),
        scratch_shapes=[spec for _, spec in scratch()],
        compiler_params=pltpu.CompilerParams(
            collective_id=0, has_side_effects=True, vmem_limit_bytes=56 << 20
        ),
    )(front_sizes, adjoint_rhs, panel_tiles, diag_inverse)


def solution(mesh):
    in_specs = (P("leaf", None, "panel"), P("leaf", "panel", None), P("leaf", "panel", None), P())
    out_specs = P("leaf", None, None, "panel")
    return jax.shard_map(
        per_device, mesh=mesh, in_specs=in_specs, out_specs=out_specs, check_vma=False
    )
```

time: 929 us -> 92.9 us (0.10)
  waiting for transfers between devices: 860 us -> 0 us
  Pallas kernels: 0 us -> 91 us
  local copies, waits for them, and re-layouts: 33.5 us -> 1.72 us
  matrix products: 15.8 us -> 0 us
  between operations: 13.5 us -> 0.01 us
    psum x5 -> x0, waiting for transfers between devices: 756 us -> none  [per_device(): summed = lax.psum(slots, ('leaf', 'panel'))]
    pallas_call x0 -> x1, Pallas kernels: none -> 91 us  [per_device(): pl.pallas_call(kernel, name='solve', out_shape=jax.ShapeDtypeStruct((1, L...]
    unnamed x11 -> x0, waiting for transfers between devices: 52.2 us -> none
    reduce_scatter x2 -> x0, waiting for transfers between devices: 51.4 us -> none  [per_device(): lax.psum_scatter(partial_value, 'panel', scatter_dimension=1, tiled=True)]
    unnamed x23 -> x1, local copies, waits for them, and re-layouts: 15.8 us -> 1.72 us
    dot_general x8 -> x0, matrix products: 14 us -> none  [the longest x5 7.32 us: per_device(): terms = jnp.dot(resid_low, factor, preferred_element_type=jnp.float32)]
  transfers between devices with their start and end apart: 9 -> 0, of which waited for: 9 -> 0; matrix products, arithmetic and copies ran while one was open for 2% -> 0% of each run, Pallas kernels for 0% -> 0%
where the time goes in v1:
time: 92.9 us; the launch traced here: 92.7 us
  Pallas kernels  91 us (98%)
  local copies, waits for them, and re-layouts  1.72 us (2%)
    pallas_call x1, Pallas kernels, per_device(): pl.pallas_call(kernel, name='solve', out_shape=jax.ShapeDtypeStruct((1, L...  91 us

profile of v1, /device:TPU:1, one launch (start us, length us, event | category | flops | bytes accessed | tf_op | source)
XLA Modules:
  0.0 92.7 jit_solution(1993161451218599380)
XLA Ops:
  0.0 91.0 %solve.1 = f32[1,5,64,256]{3,2,1,0:T(8,128)} custom-call(s32[31]{0:T(128)} %refs_0_.1, f32[1,64,496]{2,1,0:T(8,128)} %refs_1_.1, bf16[1,256,12544]{2,1,0:T(8,128)(2,1)} %refs_2_.1, bf16[1,496,2048]{2,1,0:T(8,128)(2,1)} %refs_3_.1), custom_call_target="tpu_custom_call" | custom-call | tf_op jit(solution)/shard_map/solve/pallas_call | solution.py:369
  91.0 1.7 %copy.6 = f32[1,5,64,256]{3,2,1,0:T(8,128)} copy(f32[1,5,64,256]{3,2,1,0:T(8,128)} %solve.1) | data formatting | bytes 655360
